TPU v7x, 128 devices: a whole 4x4x4 slice. The times are simulated.
128 devices in a mesh: tile: 8 (over z_lo, x), blk: 16 (over y, z_hi, core).
Axes of the slice: x: 4, y: 4, z: 4 (z_hi: 2, z_lo: 2; z = z_hi * 2 + z_lo), core: 2. Of those that a mesh axis runs over, the one named last changes fastest.
Arguments:
- tiles: bfloat16 [6144, 8, 8, 2048], P(('blk', 'tile')), may hold values from -10 to 10
- w_reduce: bfloat16 [2048, 512], replicated, may hold values from -0.125 to 0.125
- w_spatial: bfloat16 [9, 512, 512], replicated, may hold values from -0.09375 to 0.09375
- w_expand: bfloat16 [512, 2048], replicated, may hold values from -0.25 to 0.25
- w_embed: bfloat16 [2048, 1536], replicated, may hold values from -0.125 to 0.125
- w_query: bfloat16 [1536, 1536], P(None, 'tile'), may hold values from -8 to 8
- w_key: bfloat16 [1536, 1536], P(None, 'tile'), may hold values from -200 to 200
- w_value: bfloat16 [1536, 1536], P(None, 'tile'), may hold values from -0.15625 to 0.15625
- w_out: bfloat16 [1536, 1536], P('tile'), may hold values from -0.15625 to 0.15625
- slide_tiles: int32 [4], replicated, may hold values from 1 to 4608, 6144 in all
Outputs:
- mixed: bfloat16 [6144, 1536], P(('blk', 'tile'))
Inputs may be any that keep to these rules, and one draw needn't show every extreme that they name: `slide_tiles`: the counts sum to 6144 and the largest is exactly 4608.
All inputs are finite; a program needn't handle non-finite values.
Results may differ from a plain program's by a relative error of at most 0.017.
Values may be sent and summed in bfloat16 or wider, within the bound.
A program may use at most 256 MiB of HBM per device.

v0:
```python
import math
import jax
import jax.numpy as jnp
from jax import lax
from jax.sharding import PartitionSpec as P

C = 2048
MID = 512
SIDE = 8
HD = 96


def encode(block, w_reduce, w_spatial, w_expand, w_embed):
    count = block.shape[0]
    flat = block.reshape(count * SIDE * SIDE, C)
    reduced = jax.nn.relu(jnp.dot(flat, w_reduce, preferred_element_type=jnp.float32)).astype(
        jnp.bfloat16
    )
    reduced = reduced.reshape(count, SIDE, SIDE, MID)
    padded = jnp.pad(reduced, ((0, 0), (1, 1), (1, 1), (0, 0)))
    summed = jnp.zeros((count * SIDE * SIDE, MID), jnp.float32)
    for tap in range(9):
        row_off = tap // 3
        col_off = tap % 3
        window = padded[:, row_off : row_off + SIDE, col_off : col_off + SIDE, :].reshape(
            count * SIDE * SIDE, MID
        )
        summed = summed + jnp.dot(window, w_spatial[tap], preferred_element_type=jnp.float32)
    spatial = jax.nn.relu(summed).astype(jnp.bfloat16)
    output = jax.nn.relu(
        flat.astype(jnp.float32) + jnp.dot(spatial, w_expand, preferred_element_type=jnp.float32)
    )
    pooled = (jnp.sum(output.reshape(count, SIDE * SIDE, C), axis=1) / (SIDE * SIDE)).astype(
        jnp.bfloat16
    )
    return jnp.dot(pooled, w_embed, preferred_element_type=jnp.float32).astype(jnp.bfloat16)


def normalize(rows):
    values = rows.astype(jnp.float32)
    center = jnp.mean(values, axis=1, keepdims=True)
    spread = jnp.mean((values - center) ** 2, axis=1, keepdims=True)
    return ((values - center) * lax.rsqrt(spread + 1e-05)).astype(jnp.bfloat16)


def slide_of(positions, slide_tiles):
    ends = jnp.cumsum(slide_tiles)[:-1]
    return jnp.sum((positions[:, None] >= ends[None, :]).astype(jnp.int32), axis=1)


def shards(
    tiles, w_reduce, w_spatial, w_expand, w_embed, w_query, w_key, w_value, w_out, slide_tiles
):
    emb = encode(tiles, w_reduce, w_spatial, w_expand, w_embed)
    width = w_query.shape[1]
    heads_here = width // HD
    w_joined = jnp.concatenate([w_query, w_key, w_value], axis=1)
    joined = jnp.dot(
        normalize(lax.all_gather(emb, "tile", axis=0, tiled=True)),
        w_joined,
        preferred_element_type=jnp.float32,
    ).astype(jnp.bfloat16)
    length = joined.shape[0]
    query = joined[:, :width].reshape(length, heads_here, HD)
    key_value = joined[:, width:]
    query_pos = lax.axis_index("blk") * length + jnp.arange(length, dtype=jnp.int32)
    query_slide = slide_of(query_pos, slide_tiles)
    scale = 1.0 / math.sqrt(HD)
    piece = lax.all_gather(key_value, "blk", axis=0, tiled=True)
    rows = piece.shape[0]
    key_pos = jnp.arange(rows, dtype=jnp.int32)
    same = query_slide[:, None] == slide_of(key_pos, slide_tiles)[None, :]
    top_old = jnp.full((heads_here, length), -1e30, jnp.float32)
    keys = piece[:, :width].reshape(rows, heads_here, HD)
    values = piece[:, width:].reshape(rows, heads_here, HD)
    scores = jnp.einsum("qhd,khd->hqk", query, keys, preferred_element_type=jnp.float32) * scale
    scores = jnp.where(same[None], scores, -1e30)
    top_new = jnp.maximum(top_old, jnp.max(scores, axis=2))
    probs = jnp.where(same[None], jnp.exp(scores - top_new[:, :, None]), 0.0)
    total_new = jnp.sum(probs, axis=2)
    accum_new = jnp.einsum(
        "hqk,khd->hqd", probs.astype(jnp.bfloat16), values, preferred_element_type=jnp.float32
    )
    attended = (
        (accum_new / total_new[:, :, None])
        .transpose(1, 0, 2)
        .reshape(length, width)
        .astype(jnp.bfloat16)
    )
    summed = lax.psum_scatter(
        jnp.dot(attended, w_out, preferred_element_type=jnp.float32).astype(jnp.bfloat16),
        "tile",
        scatter_dimension=0,
        tiled=True,
    ).astype(jnp.float32)
    return (emb.astype(jnp.float32) + summed).astype(jnp.bfloat16)


def solution(mesh):
    placed = (
        P(("blk", "tile"), None, None, None),
        P(),
        P(),
        P(),
        P(),
        P(None, "tile"),
        P(None, "tile"),
        P(None, "tile"),
        P("tile", None),
        P(),
    )
    return jax.shard_map(
        shards, mesh=mesh, in_specs=placed, out_specs=P(("blk", "tile"), None), check_vma=False
    )
```

profile of v0, /device:TPU:0, one launch (start us, length us, event | category | flops | bytes accessed | tf_op | source)
XLA Modules:
  0.0 305.9 jit_solution(4576410972492332639)
XLA Ops:
  6.5 13.1 %maximum_convert_fusion.1 = bf16[3072,512]{1,0:T(8,128)(2,1)} fusion(bf16[3072,2048]{1,0:T(8,128)(2,1)} %bitcast.73, bf16[2048,512]{1,0:T(8,128)(2,1)} %param.11), kind=kOutput, calls=%fused_computation.17 | convolution fusion | flops 6445596672 | bytes 17825792 | tf_op jit(solution)/shard_map/dot_general | solution.py:16
  19.6 13.5 %pad_slice_fusion = (bf16[48,8,8,512]{3,2,1,0:T(8,128)(2,1)}, bf16[48,8,8,512]{3,2,1,0:T(8,128)(2,1)S(1)}, bf16[48,8,8,512]{3,2,1,0:T(8,128)(2,1)S(1)}, bf16[48,...) fusion(bf16[48,8,8,512]{3,2,1,0:T(8,128)(2,1)} %bitcast.83), kind=kLoop, calls=%fused_computation.3 | loop fusion | bytes 28311552 | tf_op jit(solution)/shard_map/slice | solution.py:25
  33.2 6.6 %fusion.40 = f32[3072,512]{1,0:T(8,128)} fusion(bf16[3072,512]{1,0:T(8,128)(2,1)} %maximum_convert_fusion.1, bf16[9,512,512]{2,1,0:T(8,128)(2,1)} %param.12), kind=kOutput, calls=%fused_computation.46 | convolution fusion | flops 1610612736 | bytes 9961472 | tf_op jit(solution)/shard_map/dot_general | solution.py:28
  39.8 4.5 %fusion.34 = f32[3072,512]{1,0:T(8,128)} fusion(bf16[3072,512]{1,0:T(8,128)(2,1)S(1)} %bitcast.82, bf16[9,512,512]{2,1,0:T(8,128)(2,1)S(1)} %copy-done.4), kind=kOutput, calls=%fused_computation.40 | convolution fusion | flops 1610612736 | bytes 9961472 | tf_op jit(solution)/shard_map/dot_general | solution.py:28
  44.3 4.5 %fusion.36 = f32[3072,512]{1,0:T(8,128)} fusion(bf16[3072,512]{1,0:T(8,128)(2,1)S(1)} %bitcast.81, bf16[9,512,512]{2,1,0:T(8,128)(2,1)S(1)} %copy-done.4), kind=kOutput, calls=%fused_computation.42 | convolution fusion | flops 1610612736 | bytes 9961472 | tf_op jit(solution)/shard_map/dot_general | solution.py:28
  48.8 4.4 %fusion.38 = f32[3072,512]{1,0:T(8,128)} fusion(bf16[3072,512]{1,0:T(8,128)(2,1)S(1)} %bitcast.80, bf16[9,512,512]{2,1,0:T(8,128)(2,1)S(1)} %copy-done.4), kind=kOutput, calls=%fused_computation.44 | convolution fusion | flops 1610612736 | bytes 9961472 | tf_op jit(solution)/shard_map/dot_general | solution.py:28
  53.2 4.4 %fusion.42 = f32[3072,512]{1,0:T(8,128)} fusion(bf16[3072,512]{1,0:T(8,128)(2,1)S(1)} %bitcast.79, bf16[9,512,512]{2,1,0:T(8,128)(2,1)S(1)} %copy-done.4), kind=kOutput, calls=%fused_computation.48 | convolution fusion | flops 1610612736 | bytes 9961472 | tf_op jit(solution)/shard_map/dot_general | solution.py:28
  57.7 4.5 %fusion.44 = f32[3072,512]{1,0:T(8,128)} fusion(bf16[3072,512]{1,0:T(8,128)(2,1)S(1)} %bitcast.78, bf16[9,512,512]{2,1,0:T(8,128)(2,1)S(1)} %copy-done.4), kind=kOutput, calls=%fused_computation.50 | convolution fusion | flops 1610612736 | bytes 9961472 | tf_op jit(solution)/shard_map/dot_general | solution.py:28
  62.1 4.4 %fusion.46 = f32[3072,512]{1,0:T(8,128)} fusion(bf16[3072,512]{1,0:T(8,128)(2,1)S(1)} %bitcast.77, bf16[9,512,512]{2,1,0:T(8,128)(2,1)S(1)} %copy-done.4), kind=kOutput, calls=%fused_computation.52 | convolution fusion | flops 1610612736 | bytes 9961472 | tf_op jit(solution)/shard_map/dot_general | solution.py:28
  66.6 4.5 %fusion.48 = f32[3072,512]{1,0:T(8,128)} fusion(bf16[3072,512]{1,0:T(8,128)(2,1)S(1)} %bitcast.76, bf16[9,512,512]{2,1,0:T(8,128)(2,1)S(1)} %copy-done.4), kind=kOutput, calls=%fused_computation.54 | convolution fusion | flops 1610612736 | bytes 9961472 | tf_op jit(solution)/shard_map/dot_general | solution.py:28
  71.0 33.0 %add_maximum_fusion = f32[3072,2048]{1,0:T(8,128)} fusion(bf16[3072,2048]{1,0:T(8,128)(2,1)} %bitcast.74, bf16[512,2048]{1,0:T(8,128)(2,1)S(1)} %copy-done, f32[3072,512]{1,0:T(8,128)} %fusion.34, f32[3072,512]{1,0:T(8,128)} %fusion.36, f32[3072,512]{1,0:T(8,128)} %fusion.38, f32[3072,512]{1,0:T(8,128)} %fusion.40, f32[3072,512]{1,0:T(8,128)} %fusion.42, ...), kind=kOutput, calls=%fused_computation | convolution fusion | flops 8087666688 | bytes 93847552 | tf_op jit(solution)/shard_map/dot_general | solution.py:31
  104.0 9.5 %reduce_sum.54 = f32[48,2048]{1,0:T(8,128)S(1)} reduce(f32[48,64,2048]{2,1,0:T(8,128)} %bitcast.72, f32[]{:T(128)} %constant.11.clone.1), dimensions={1}, to_apply=%region_0.1 | reduce | flops 6193152 | bytes 25559044 | tf_op jit(solution)/shard_map/reduce_sum | solution.py:33
  113.6 4.7 %convolution_convert_fusion.1 = bf16[48,1536]{1,0:T(8,128)(2,1)} fusion(bf16[2048,1536]{1,0:T(8,128)(2,1)} %param.14, f32[48,2048]{1,0:T(8,128)S(1)} %reduce_sum.54), kind=kOutput, calls=%fused_computation.26 | convolution fusion | flops 302260224 | bytes 6832128 | tf_op jit(solution)/shard_map/dot_general | solution.py:36
  118.3 0.0 all-gather.5.cloned.1.call-start
  118.4 41.8 %all-gather.3.cloned.1.call-done = bf16[384,1536]{1,0:T(8,128)(2,1)} async-done(((bf16[48,1536]{1,0:T(8,128)(2,1)}), bf16[384,1536]{1,0:T(8,128)(2,1)}) %all-gather.3.cloned.1.call-update) | async-done | bytes 1179664 | tf_op jit(solution)/shard_map/all_gather | solution.py:59
  160.2 1.5 convert_reduce_fusion
  161.7 1.7 fusion.8
  163.5 2.5 fusion.16
  166.0 0.7 slice.92
  166.7 0.0 reduce-scatter.2.cloned.1.call-start
  166.8 0.2 reduce-window.4
  167.0 0.1 convert_reduce_fusion.2
  167.1 0.1 convert_reduce_fusion.1
  167.2 2.9 broadcast_compare_fusion
  170.1 57.6 %all-gather.5.cloned.1.call-done = bf16[6144,384]{0,1:T(8,128)(2,1)} async-done(((bf16[384,384]{0,1:T(8,128)(2,1)}), bf16[6144,384]{0,1:T(8,128)(2,1)}) %all-gather.5.cloned.1.call-update) | async-done | bytes 4718608 | tf_op jit(solution)/shard_map/all_gather | solution.py:69
  227.7 5.1 %fusion.67 = (bf16[6144,192]{0,1:T(8,128)(2,1)}, bf16[6144,192]{0,1:T(8,128)(2,1)}) fusion(bf16[6144,384]{0,1:T(8,128)(2,1)} %all-gather.5.cloned.1.call-done), kind=kLoop, calls=%fused_computation.82 | loop fusion | bytes 9437184 | tf_op jit(solution)/shard_map/slice | solution.py:74
  232.8 6.4 %fusion = (f32[2,384]{1,0:T(2,128)S(1)}, f32[2,384,6144]{2,1,0:T(8,128)S(1)}) fusion(pred[384,6144]{1,0:T(8,128)(4,1)} %broadcast_compare_fusion, bf16[384,2,96]{0,2,1:T(8,128)(2,1)S(1)} %bitcast.86, bf16[6144,2,96]{0,2,1:T(8,128)(2,1)} %bitcast.85), kind=kOutput, calls=%fused_computation.11 | convolution fusion | flops 920124672 | bytes 23743488 | tf_op jit(solution)/shard_map/qhd,khd->hqk/dot_general | solution.py:76
  239.2 8.0 %fusion.1 = f32[2,384]{1,0:T(2,128)S(1)} fusion(f32[2,384,6144]{2,1,0:T(8,128)S(1)} %get-tuple-element.16, f32[2,384]{1,0:T(2,128)S(1)} %broadcast_maximum_fusion, pred[384,6144]{1,0:T(8,128)(4,1)} %broadcast_compare_fusion), kind=kLoop, calls=%fused_computation.12 | loop fusion | flops 23592192 | bytes 21239808 | tf_op jit(solution)/shard_map/reduce_sum | solution.py:80
  247.2 10.9 %fusion.28 = bf16[384,2,96]{0,2,1:T(8,128)(2,1)S(1)} fusion(bf16[6144,2,96]{0,2,1:T(8,128)(2,1)} %bitcast.84, f32[2,384,6144]{2,1,0:T(8,128)} %copy-done.2, f32[2,384]{1,0:T(2,128)S(1)} %broadcast_maximum_fusion, pred[384,6144]{1,0:T(8,128)(4,1)} %broadcast_compare_fusion, f32[384,2]{0,1:T(2,128)S(1)} %bitcast.88), kind=kOutput, calls=%fused_computation.38 | convolution fusion | flops 929710080 | bytes 23746560 | tf_op jit(solution)/shard_map/hqk,khd->hqd/dot_general | solution.py:81
  258.1 1.5 convolution_convert_fusion
  259.7 38.1 %reduce-scatter.2.cloned.1.call-done = bf16[48,1536]{1,0:T(8,128)(2,1)} async-done(((bf16[384,1536]{1,0:T(8,128)(2,1)}), bf16[48,1536]{1,0:T(8,128)(2,1)}) %reduce-scatter.2.cloned.1.call-update) | async-done | bytes 147472 | tf_op jit(solution)/shard_map/reduce_scatter | solution.py:90
  297.8 1.6 add_convert_fusion
  (32 shorter events, 0.2 us)
Async XLA Ops:
  6.5 64.5 %copy-start = (bf16[512,2048]{1,0:T(8,128)(2,1)S(1)}, bf16[512,2048]{1,0:T(8,128)(2,1)}, u32[]{:S(2)}) copy-start(bf16[512,2048]{1,0:T(8,128)(2,1)} %param.13) | copy-start | bytes 6291460
  6.5 153.6 %all-gather.3.cloned.1.call-start = ((), (), s32[]{:S(2)}) async-start(), calls=%async_computation.1 | async-start | bytes 1327104 | tf_op jit(solution)/shard_map/all_gather | solution.py:59
  33.1 6.7 %copy-start.3 = (bf16[48,8,8,512]{3,2,1,0:T(8,128)(2,1)S(1)}, bf16[48,8,8,512]{3,2,1,0:T(8,128)(2,1)}, u32[]{:S(2)}) copy-start(bf16[48,8,8,512]{3,2,1,0:T(8,128)(2,1)} %get-tuple-element.13) | copy-start | bytes 9437188
  33.1 6.7 %copy-start.4 = (bf16[9,512,512]{2,1,0:T(8,128)(2,1)S(1)}, bf16[9,512,512]{2,1,0:T(8,128)(2,1)}, u32[]{:S(2)}) copy-start(bf16[9,512,512]{2,1,0:T(8,128)(2,1)} %param.12) | copy-start | bytes 14155780
  113.6 49.9 %copy-start.7 = (bf16[1536,192]{0,1:T(8,128)(2,1)S(1)}, bf16[1536,192]{0,1:T(8,128)(2,1)}, u32[]{:S(2)}) copy-start(bf16[1536,192]{0,1:T(8,128)(2,1)} %param.17) | copy-start | bytes 1769476
  113.6 49.8 %copy-start.8 = (bf16[1536,192]{0,1:T(8,128)(2,1)S(1)}, bf16[1536,192]{0,1:T(8,128)(2,1)}, u32[]{:S(2)}) copy-start(bf16[1536,192]{0,1:T(8,128)(2,1)} %param.16) | copy-start | bytes 1769476
  113.6 49.8 %copy-start.9 = (bf16[1536,192]{0,1:T(8,128)(2,1)S(1)}, bf16[1536,192]{0,1:T(8,128)(2,1)}, u32[]{:S(2)}) copy-start(bf16[1536,192]{0,1:T(8,128)(2,1)} %param.15) | copy-start | bytes 1769476
  118.3 109.3 %all-gather.5.cloned.1.call-start = ((), (), s32[]{:S(2)}) async-start(), calls=%async_computation.2 | async-start | bytes 5013504 | tf_op jit(solution)/shard_map/all_gather | solution.py:69
  163.4 3.3 %copy-start.10 = (s32[4]{0:T(128)S(1)}, s32[4]{0:T(128)}, u32[]{:S(2)}) copy-start(s32[4]{0:T(128)} %param.19) | copy-start | bytes 52
  166.7 131.1 %reduce-scatter.2.cloned.1.call-start = ((), (), s32[]{:S(2)}) async-start(), calls=%async_computation.3 | async-start | bytes 1327104 | tf_op jit(solution)/shard_map/reduce_scatter | solution.py:90
  239.2 8.0 %copy-start.2 = (f32[2,384,6144]{2,1,0:T(8,128)}, f32[2,384,6144]{2,1,0:T(8,128)S(1)}, u32[]{:S(2)}) copy-start(f32[2,384,6144]{2,1,0:T(8,128)S(1)} %get-tuple-element.16) | copy-start | bytes 56623108
  247.2 10.9 %copy-start.6 = (bf16[192,1536]{1,0:T(8,128)(2,1)S(1)}, bf16[192,1536]{1,0:T(8,128)(2,1)}, u32[]{:S(2)}) copy-start(bf16[192,1536]{1,0:T(8,128)(2,1)} %param.18) | copy-start | bytes 1769476
  247.2 50.6 %copy-start.5 = (bf16[48,1536]{1,0:T(8,128)(2,1)S(1)}, bf16[48,1536]{1,0:T(8,128)(2,1)}, u32[]{:S(2)}) copy-start(bf16[48,1536]{1,0:T(8,128)(2,1)} %convolution_convert_fusion.1) | copy-start | bytes 442372
  247.2 52.2 %copy-start.1 = (bf16[512,2048]{1,0:T(8,128)(2,1)S(1)}, bf16[512,2048]{1,0:T(8,128)(2,1)}, u32[]{:S(2)}) copy-start(bf16[512,2048]{1,0:T(8,128)(2,1)} %param.13) | copy-start | bytes 6291460
Sparse Core Ops, SparseCore 0:
  118.4 41.6 all-gather.2
  166.8 60.7 all-gather.4
  259.8 37.9 reduce-scatter.1
where the time goes:
time: 306 us
  waiting for transfers between devices  138 us (45%)
  matrix products  110 us (36%)
  other arithmetic  25.6 us (8%)
  local copies, waits for them, and re-layouts  19.4 us (6%)
  between operations  13.3 us (4%)
    all_gather x1, waiting for transfers between devices, shards(): piece = lax.all_gather(key_value, 'blk', axis=0, tiled=True)  57.6 us
    all_gather x1, waiting for transfers between devices, shards(): lax.all_gather(emb, 'tile', axis=0, tiled=True)  41.8 us
    reduce_scatter x1, waiting for transfers between devices, shards(): lax.psum_scatter(jnp.dot(attended, w_out, preferred_element_type=jnp.floa...  38.1 us
    dot_general x8, matrix products, encode(): jnp.dot(window, w_spatial[tap], preferred_element_type=jnp.float32)  37.9 us
    dot_general x1, matrix products, encode(): jnp.dot(spatial, w_expand, preferred_element_type=jnp.float32)  33 us
    slice x1, local copies, waits for them, and re-layouts, encode(): padded[:, row_off:row_off + SIDE, col_off:col_off + SIDE, :]  13.5 us
    dot_general x1, matrix products, encode(): jnp.dot(flat, w_reduce, preferred_element_type=jnp.float32)  13.1 us
    dot_general x1, matrix products, shards(): jnp.einsum('hqk,khd->hqd', probs.astype(jnp.bfloat16), values, preferred_...  10.9 us
  transfers between devices with their start and end apart: 3, of which 3 were waited for; matrix products, arithmetic and copies ran while one was open for 1% of the time, Pallas kernels for 0%

commit v1 on v0

--- a/solution.py
+++ b/solution.py
@@ -56,7 +56,11 @@
     heads_here = width // HD
     w_joined = jnp.concatenate([w_query, w_key, w_value], axis=1)
     joined = jnp.dot(
-        normalize(lax.all_gather(emb, "tile", axis=0, tiled=True)),
+        normalize(
+            jnp.concatenate(
+                lax.all_to_all(jnp.stack([emb] * lax.axis_size("tile")), "tile", 0, 0), axis=0
+            )
+        ),
         w_joined,
         preferred_element_type=jnp.float32,
     ).astype(jnp.bfloat16)

time: 306 us -> 285 us (0.931)
  waiting for transfers between devices: 138 us -> 96.9 us
  blocking collectives: 0 us -> 22.8 us
    all_gather x1 -> x0, waiting for transfers between devices: 41.8 us -> none  [shards(): lax.all_gather(emb, 'tile', axis=0, tiled=True)]
    all_to_all x0 -> x1, blocking collectives: none -> 22.8 us  [shards(): lax.all_to_all(jnp.stack([emb] * lax.axis_size('tile')), 'tile', 0, 0)]
  transfers between devices with their start and end apart: 3 -> 2, of which waited for: 3 -> 2; matrix products, arithmetic and copies ran while one was open for 1% -> 1% of each run, Pallas kernels for 0% -> 0%
where the time goes in v1:
time: 285 us; the launch traced here: 284 us
  matrix products  108 us (38%)
  waiting for transfers between devices  96.9 us (34%)
  other arithmetic  23.4 us (8%)
  blocking collectives  22.8 us (8%)
  local copies, waits for them, and re-layouts  19.7 us (7%)
  between operations  13.6 us (5%)
    all_gather x1, waiting for transfers between devices, shards(): piece = lax.all_gather(key_value, 'blk', axis=0, tiled=True)  58.8 us
    reduce_scatter x1, waiting for transfers between devices, shards(): lax.psum_scatter(jnp.dot(attended, w_out, preferred_element_type=jnp.floa...  38 us
    dot_general x8, matrix products, encode(): jnp.dot(window, w_spatial[tap], preferred_element_type=jnp.float32)  37.9 us
    dot_general x1, matrix products, encode(): jnp.dot(spatial, w_expand, preferred_element_type=jnp.float32)  33 us
    all_to_all x1, blocking collectives, shards(): lax.all_to_all(jnp.stack([emb] * lax.axis_size('tile')), 'tile', 0, 0)  22.8 us
    slice x1, local copies, waits for them, and re-layouts, encode(): padded[:, row_off:row_off + SIDE, col_off:col_off + SIDE, :]  13.5 us
    dot_general x1, matrix products, encode(): jnp.dot(flat, w_reduce, preferred_element_type=jnp.float32)  13.1 us
    dot_general x1, matrix products, shards(): jnp.einsum('hqk,khd->hqd', probs.astype(jnp.bfloat16), values, preferred_...  10.9 us
  transfers between devices with their start and end apart: 2, of which 2 were waited for; matrix products, arithmetic and copies ran while one was open for 1% of the time, Pallas kernels for 0%

profile of v1, /device:TPU:0, one launch (start us, length us, event | category | flops | bytes accessed | tf_op | source)
XLA Modules:
  0.0 284.2 jit_solution(17905265183496924)
XLA Ops:
  6.5 13.1 %maximum_convert_fusion.1 = bf16[3072,512]{1,0:T(8,128)(2,1)} fusion(bf16[3072,2048]{1,0:T(8,128)(2,1)} %bitcast.80, bf16[2048,512]{1,0:T(8,128)(2,1)} %param.11), kind=kOutput, calls=%fused_computation.17 | convolution fusion | flops 6445596672 | bytes 17825792 | tf_op jit(solution)/shard_map/dot_general | solution.py:16
  19.6 13.5 %pad_slice_fusion = (bf16[48,8,8,512]{3,2,1,0:T(8,128)(2,1)}, bf16[48,8,8,512]{3,2,1,0:T(8,128)(2,1)S(1)}, bf16[48,8,8,512]{3,2,1,0:T(8,128)(2,1)S(1)}, bf16[48,...) fusion(bf16[48,8,8,512]{3,2,1,0:T(8,128)(2,1)} %bitcast.90), kind=kLoop, calls=%fused_computation.3 | loop fusion | bytes 28311552 | tf_op jit(solution)/shard_map/slice | solution.py:25
  33.2 6.6 %fusion.35 = f32[3072,512]{1,0:T(8,128)} fusion(bf16[3072,512]{1,0:T(8,128)(2,1)} %maximum_convert_fusion.1, bf16[9,512,512]{2,1,0:T(8,128)(2,1)} %param.12), kind=kOutput, calls=%fused_computation.43 | convolution fusion | flops 1610612736 | bytes 9961472 | tf_op jit(solution)/shard_map/dot_general | solution.py:28
  39.8 4.5 %fusion.29 = f32[3072,512]{1,0:T(8,128)} fusion(bf16[3072,512]{1,0:T(8,128)(2,1)S(1)} %bitcast.89, bf16[9,512,512]{2,1,0:T(8,128)(2,1)S(1)} %copy-done.4), kind=kOutput, calls=%fused_computation.37 | convolution fusion | flops 1610612736 | bytes 9961472 | tf_op jit(solution)/shard_map/dot_general | solution.py:28
  44.3 4.5 %fusion.31 = f32[3072,512]{1,0:T(8,128)} fusion(bf16[3072,512]{1,0:T(8,128)(2,1)S(1)} %bitcast.88, bf16[9,512,512]{2,1,0:T(8,128)(2,1)S(1)} %copy-done.4), kind=kOutput, calls=%fused_computation.39 | convolution fusion | flops 1610612736 | bytes 9961472 | tf_op jit(solution)/shard_map/dot_general | solution.py:28
  48.8 4.4 %fusion.33 = f32[3072,512]{1,0:T(8,128)} fusion(bf16[3072,512]{1,0:T(8,128)(2,1)S(1)} %bitcast.87, bf16[9,512,512]{2,1,0:T(8,128)(2,1)S(1)} %copy-done.4), kind=kOutput, calls=%fused_computation.41 | convolution fusion | flops 1610612736 | bytes 9961472 | tf_op jit(solution)/shard_map/dot_general | solution.py:28
  53.2 4.4 %fusion.37 = f32[3072,512]{1,0:T(8,128)} fusion(bf16[3072,512]{1,0:T(8,128)(2,1)S(1)} %bitcast.86, bf16[9,512,512]{2,1,0:T(8,128)(2,1)S(1)} %copy-done.4), kind=kOutput, calls=%fused_computation.45 | convolution fusion | flops 1610612736 | bytes 9961472 | tf_op jit(solution)/shard_map/dot_general | solution.py:28
  57.7 4.5 %fusion.39 = f32[3072,512]{1,0:T(8,128)} fusion(bf16[3072,512]{1,0:T(8,128)(2,1)S(1)} %bitcast.85, bf16[9,512,512]{2,1,0:T(8,128)(2,1)S(1)} %copy-done.4), kind=kOutput, calls=%fused_computation.47 | convolution fusion | flops 1610612736 | bytes 9961472 | tf_op jit(solution)/shard_map/dot_general | solution.py:28
  62.1 4.4 %fusion.41 = f32[3072,512]{1,0:T(8,128)} fusion(bf16[3072,512]{1,0:T(8,128)(2,1)S(1)} %bitcast.84, bf16[9,512,512]{2,1,0:T(8,128)(2,1)S(1)} %copy-done.4), kind=kOutput, calls=%fused_computation.49 | convolution fusion | flops 1610612736 | bytes 9961472 | tf_op jit(solution)/shard_map/dot_general | solution.py:28
  66.6 4.5 %fusion.43 = f32[3072,512]{1,0:T(8,128)} fusion(bf16[3072,512]{1,0:T(8,128)(2,1)S(1)} %bitcast.83, bf16[9,512,512]{2,1,0:T(8,128)(2,1)S(1)} %copy-done.4), kind=kOutput, calls=%fused_computation.51 | convolution fusion | flops 1610612736 | bytes 9961472 | tf_op jit(solution)/shard_map/dot_general | solution.py:28
  71.0 33.0 %add_maximum_fusion = f32[3072,2048]{1,0:T(8,128)} fusion(bf16[3072,2048]{1,0:T(8,128)(2,1)} %bitcast.81, bf16[512,2048]{1,0:T(8,128)(2,1)S(1)} %copy-done, f32[3072,512]{1,0:T(8,128)} %fusion.29, f32[3072,512]{1,0:T(8,128)} %fusion.31, f32[3072,512]{1,0:T(8,128)} %fusion.33, f32[3072,512]{1,0:T(8,128)} %fusion.35, f32[3072,512]{1,0:T(8,128)} %fusion.37, ...), kind=kOutput, calls=%fused_computation | convolution fusion | flops 8087666688 | bytes 93847552 | tf_op jit(solution)/shard_map/dot_general | solution.py:31
  104.0 9.5 %reduce_sum.54 = f32[48,2048]{1,0:T(8,128)S(1)} reduce(f32[48,64,2048]{2,1,0:T(8,128)} %bitcast.79, f32[]{:T(128)} %constant.11.clone.1), dimensions={1}, to_apply=%region_0.1 | reduce | flops 6193152 | bytes 25559044 | tf_op jit(solution)/shard_map/reduce_sum | solution.py:33
  113.6 3.9 %convolution_convert_fusion.1 = bf16[48,1536]{1,0:T(8,128)(2,1)S(1)} fusion(bf16[2048,1536]{1,0:T(8,128)(2,1)} %param.14, f32[48,2048]{1,0:T(8,128)S(1)} %reduce_sum.54), kind=kOutput, calls=%fused_computation.24 | convolution fusion | flops 302260224 | bytes 6832128 | tf_op jit(solution)/shard_map/dot_general | solution.py:36
  117.5 0.1 stack.2
  117.6 22.8 %all_to_all.5 = bf16[8,48,1536]{2,1,0:T(8,128)(2,1)S(1)} all-to-all(bf16[8,48,1536]{2,1,0:T(8,128)(2,1)S(1)} %stack.2), channel_id=1, replica_groups=mesh['tile'=8,'blk'=16] {'tile'}, dimensions={0} | all-to-all | bytes 2359296 | tf_op jit(solution)/shard_map/all_to_all | solution.py:61
  140.4 0.2 convert_reduce_fusion
  140.7 0.4 multiply_reduce_fusion
  141.3 0.4 fusion.7
  141.7 1.1 fusion.14
  142.8 0.7 slice.92
  143.6 0.2 reduce-window.4
  143.8 0.1 convert_reduce_fusion.2
  143.9 0.1 convert_reduce_fusion.1
  144.0 2.9 %broadcast_compare_fusion = pred[384,6144]{1,0:T(8,128)(4,1)} fusion(s32[6144]{0:T(1024)S(1)} %convert_reduce_fusion.1, s32[384]{0:T(512)S(1)} %convert_reduce_fusion.2), kind=kLoop, calls=%fused_computation.18 | loop fusion | flops 2359296 | bytes 2385408 | tf_op jit(solution)/shard_map/eq | solution.py:76
  146.9 58.8 %all-gather.2.cloned.1.call-done = bf16[6144,384]{0,1:T(8,128)(2,1)} async-done(((bf16[384,384]{0,1:T(8,128)(2,1)}), bf16[6144,384]{0,1:T(8,128)(2,1)}) %all-gather.2.cloned.1.call-update) | async-done | bytes 4718608 | tf_op jit(solution)/shard_map/all_gather | solution.py:73
  205.7 5.1 %fusion.62 = (bf16[6144,192]{0,1:T(8,128)(2,1)}, bf16[6144,192]{0,1:T(8,128)(2,1)}) fusion(bf16[6144,384]{0,1:T(8,128)(2,1)} %all-gather.2.cloned.1.call-done), kind=kLoop, calls=%fused_computation.79 | loop fusion | bytes 9437184 | tf_op jit(solution)/shard_map/slice | solution.py:78
  210.9 6.4 %fusion = (f32[2,384]{1,0:T(2,128)S(1)}, f32[2,384,6144]{2,1,0:T(8,128)S(1)}) fusion(pred[384,6144]{1,0:T(8,128)(4,1)} %broadcast_compare_fusion, bf16[384,2,96]{0,2,1:T(8,128)(2,1)S(1)} %bitcast.93, bf16[6144,2,96]{0,2,1:T(8,128)(2,1)} %bitcast.92), kind=kOutput, calls=%fused_computation.11 | convolution fusion | flops 920124672 | bytes 23743488 | tf_op jit(solution)/shard_map/qhd,khd->hqk/dot_general | solution.py:80
  217.2 8.0 %fusion.1 = f32[2,384]{1,0:T(2,128)S(1)} fusion(f32[2,384,6144]{2,1,0:T(8,128)S(1)} %get-tuple-element.16, f32[2,384]{1,0:T(2,128)S(1)} %broadcast_maximum_fusion, pred[384,6144]{1,0:T(8,128)(4,1)} %broadcast_compare_fusion), kind=kLoop, calls=%fused_computation.12 | loop fusion | flops 23592192 | bytes 21239808 | tf_op jit(solution)/shard_map/reduce_sum | solution.py:84
  225.3 10.9 %fusion.23 = bf16[384,2,96]{0,2,1:T(8,128)(2,1)S(1)} fusion(bf16[6144,2,96]{0,2,1:T(8,128)(2,1)} %bitcast.91, f32[2,384,6144]{2,1,0:T(8,128)} %copy-done.2, f32[2,384]{1,0:T(2,128)S(1)} %broadcast_maximum_fusion, pred[384,6144]{1,0:T(8,128)(4,1)} %broadcast_compare_fusion, f32[384,2]{0,1:T(2,128)S(1)} %bitcast.95), kind=kOutput, calls=%fused_computation.35 | convolution fusion | flops 929710080 | bytes 23746560 | tf_op jit(solution)/shard_map/hqk,khd->hqd/dot_general | solution.py:85
  236.2 1.5 convolution_convert_fusion
  237.7 38.0 %reduce-scatter.2.cloned.1.call-done = bf16[48,1536]{1,0:T(8,128)(2,1)} async-done(((bf16[384,1536]{1,0:T(8,128)(2,1)}), bf16[48,1536]{1,0:T(8,128)(2,1)}) %reduce-scatter.2.cloned.1.call-update) | async-done | bytes 147472 | tf_op jit(solution)/shard_map/reduce_scatter | solution.py:94
  275.8 1.6 add_convert_fusion
  (32 shorter events, 0.3 us)
Async XLA Ops:
  6.5 64.5 %copy-start = (bf16[512,2048]{1,0:T(8,128)(2,1)S(1)}, bf16[512,2048]{1,0:T(8,128)(2,1)}, u32[]{:S(2)}) copy-start(bf16[512,2048]{1,0:T(8,128)(2,1)} %param.13) | copy-start | bytes 6291460
  6.5 199.2 %all-gather.2.cloned.1.call-start = ((), (), s32[]{:S(2)}) async-start(), calls=%async_computation.2 | async-start | bytes 5013504 | tf_op jit(solution)/shard_map/all_gather | solution.py:73
  33.1 6.7 %copy-start.3 = (bf16[48,8,8,512]{3,2,1,0:T(8,128)(2,1)S(1)}, bf16[48,8,8,512]{3,2,1,0:T(8,128)(2,1)}, u32[]{:S(2)}) copy-start(bf16[48,8,8,512]{3,2,1,0:T(8,128)(2,1)} %get-tuple-element.13) | copy-start | bytes 9437188
  33.1 6.7 %copy-start.4 = (bf16[9,512,512]{2,1,0:T(8,128)(2,1)S(1)}, bf16[9,512,512]{2,1,0:T(8,128)(2,1)}, u32[]{:S(2)}) copy-start(bf16[9,512,512]{2,1,0:T(8,128)(2,1)} %param.12) | copy-start | bytes 14155780
  117.5 24.2 %copy-start.6 = (bf16[1536,192]{0,1:T(8,128)(2,1)S(1)}, bf16[1536,192]{0,1:T(8,128)(2,1)}, u32[]{:S(2)}) copy-start(bf16[1536,192]{0,1:T(8,128)(2,1)} %param.17) | copy-start | bytes 1769476
  117.5 24.2 %copy-start.7 = (bf16[1536,192]{0,1:T(8,128)(2,1)S(1)}, bf16[1536,192]{0,1:T(8,128)(2,1)}, u32[]{:S(2)}) copy-start(bf16[1536,192]{0,1:T(8,128)(2,1)} %param.16) | copy-start | bytes 1769476
  117.5 24.2 %copy-start.8 = (bf16[1536,192]{0,1:T(8,128)(2,1)S(1)}, bf16[1536,192]{0,1:T(8,128)(2,1)}, u32[]{:S(2)}) copy-start(bf16[1536,192]{0,1:T(8,128)(2,1)} %param.15) | copy-start | bytes 1769476
  141.7 1.9 copy-start.9
  143.6 132.2 %reduce-scatter.2.cloned.1.call-start = ((), (), s32[]{:S(2)}) async-start(), calls=%async_computation.3 | async-start | bytes 1327104 | tf_op jit(solution)/shard_map/reduce_scatter | solution.py:94
  217.2 8.0 %copy-start.2 = (f32[2,384,6144]{2,1,0:T(8,128)}, f32[2,384,6144]{2,1,0:T(8,128)S(1)}, u32[]{:S(2)}) copy-start(f32[2,384,6144]{2,1,0:T(8,128)S(1)} %get-tuple-element.16) | copy-start | bytes 56623108
  225.3 10.9 %copy-start.5 = (bf16[192,1536]{1,0:T(8,128)(2,1)S(1)}, bf16[192,1536]{1,0:T(8,128)(2,1)}, u32[]{:S(2)}) copy-start(bf16[192,1536]{1,0:T(8,128)(2,1)} %param.18) | copy-start | bytes 1769476
  225.3 52.1 %copy-start.1 = (bf16[512,2048]{1,0:T(8,128)(2,1)S(1)}, bf16[512,2048]{1,0:T(8,128)(2,1)}, u32[]{:S(2)}) copy-start(bf16[512,2048]{1,0:T(8,128)(2,1)} %param.13) | copy-start | bytes 6291460
Sparse Core Ops, SparseCore 0:
  143.7 62.0 all-gather.1
  237.8 37.8 reduce-scatter.1
